TPU v7x, 32 devices: a whole 2x2x4 slice. The times are simulated.
32 devices in a mesh: gx: 16 (over z, x, core), gy: 2 (over y).
Axes of the slice: x: 2, y: 2, z: 4, core: 2. Of those that a mesh axis runs over, the one named last changes fastest.
Arguments:
- volume_field: float32 [3, 256, 32, 128], P(None, 'gx', 'gy'), may hold values from -6 to 6
- diag_blocks: float32 [3, 3, 256, 32, 128], P(None, None, 'gx', 'gy'), may hold values from -4 to 4
- face_weights: float32 [6, 2, 256, 32, 128], P(None, None, 'gx', 'gy'), may hold values from 0.3 to 3
- boundary_field: float32 [16, 2, 1536], P('gx', 'gy'), may hold values from -6 to 6
- self_term: float32 [16, 2, 1536], P('gx', 'gy'), may hold values from 0.5 to 2
- coupling: float32 [16, 2, 1536], P('gx', 'gy'), may hold values from 0.3 to 3
- owner_map: int32 [16, 2, 1536], P('gx', 'gy'), may hold values from 0 to 1535, as said below
- left_basis: bfloat16 [32, 16, 2, 1536], P('gy', 'gx'), may hold values from -1 to 1
- right_basis: bfloat16 [256, 16, 2, 1536], P('gx', None, 'gy'), may hold values from -0.0390625 to 0.0390625
Outputs:
- volume_out: float32 [3, 256, 32, 128], P(None, 'gx', 'gy')
- boundary_out: float32 [16, 2, 1536], P('gx', 'gy')
Inputs may be any that keep to these rules, and one draw needn't show every extreme that they name: `owner_map`: within each subdomain (p, q) the 1536 entries name every surface edge of that subdomain exactly once.
All inputs are finite; a program needn't handle non-finite values.
Results may differ from a plain program's by a relative error of at most 0.0017.
Values may be sent and summed in bfloat16 or wider, within the bound.
No kernel may reach another device: no remote copies, remote signals or barrier semaphores. Data moves between devices by JAX's collectives and lax.ppermute only.
A program may use at most 64 MiB of HBM per device.

v0:
```python
import jax
import jax.numpy as jnp
from jax import lax
from jax.sharding import PartitionSpec as P


def with_halo(value, sides, width):
    for axis, dim in sides:
        devices, length = (lax.axis_size(axis), value.shape[dim])
        up = [(i, (i + 1) % devices) for i in range(devices - 1)]
        down = [(j, i) for i, j in up]
        last = lax.slice_in_dim(value, length - width, length, axis=dim)
        initial = lax.slice_in_dim(value, 0, width, axis=dim)
        before = lax.ppermute(last, axis, up)
        after = lax.ppermute(initial, axis, down)
        value = jnp.concatenate([before, value, after], axis=dim)
    return value


def apply_blocks(field_in, diag_blocks, face_weights, neighbours):
    comp_rows = []
    for comp in range(3):
        accum_row = (
            diag_blocks[comp, 0] * field_in[0]
            + diag_blocks[comp, 1] * field_in[1]
            + diag_blocks[comp, 2] * field_in[2]
        )
        comp_rows.append(accum_row)
    for offset in range(6):
        direction = offset // 2
        tangent = [comp for comp in range(3) if comp != direction]
        for slot in range(2):
            comp_rows[tangent[slot]] = (
                comp_rows[tangent[slot]] - face_weights[offset, slot] * neighbours[offset][slot]
            )
    return jnp.stack(comp_rows)


def on_device(
    volume_field,
    diag_blocks,
    face_weights,
    boundary_field,
    self_term,
    coupling,
    owner_map,
    left_basis,
    right_basis,
):
    z_padded = jnp.pad(volume_field[0:2], ((0, 0), (0, 0), (0, 0), (1, 1)))
    plus_z = z_padded[..., 2:]
    minus_z = z_padded[..., :-2]
    padded = with_halo(volume_field, (("gx", 1), ("gy", 2)), 1)
    plus_x = padded[1:3, 2:, 1:-1]
    minus_x = padded[1:3, :-2, 1:-1]
    plus_y = padded[0::2, 1:-1, 2:]
    minus_y = padded[0::2, 1:-1, :-2]
    neighbours = [plus_x, minus_x, plus_y, minus_y, plus_z, minus_z]
    stiffness = apply_blocks(volume_field, diag_blocks, face_weights, neighbours)
    cells_x = volume_field.shape[1]
    cells_y = volume_field.shape[2]
    boundary_count = boundary_field.shape[2]
    surface = jnp.stack([volume_field[..., 0], volume_field[..., -1]]).reshape(boundary_count)
    owner_flat = owner_map.reshape(boundary_count)
    edge_trace = surface[owner_flat].reshape(boundary_field.shape)
    placed = (
        jnp.zeros((boundary_count,), jnp.float32)
        .at[owner_flat]
        .set((coupling * boundary_field).reshape(boundary_count))
    )
    placed = placed.reshape(2, 3, cells_x, cells_y)
    volume_out = stiffness.at[:, :, :, 0].add(placed[0]).at[:, :, :, -1].add(placed[1])
    boundary_half = boundary_field.astype(jnp.bfloat16)
    gathered = lax.all_gather(boundary_half, "gx", axis=0, tiled=True)
    coef = jnp.einsum("rxbk,xbk->r", right_basis, gathered, preferred_element_type=jnp.float32)
    coef_half = coef.astype(jnp.bfloat16)
    partial_value = jnp.einsum(
        "rabk,r->abk", left_basis, coef_half, preferred_element_type=jnp.float32
    )
    integral = lax.psum_scatter(partial_value, "gy", scatter_dimension=1, tiled=True)
    boundary_out = self_term * boundary_field + integral + coupling * edge_trace
    return (volume_out, boundary_out)


def solution(mesh):
    return jax.shard_map(
        on_device,
        mesh=mesh,
        in_specs=(
            P(None, "gx", "gy", None),
            P(None, None, "gx", "gy", None),
            P(None, None, "gx", "gy", None),
            P("gx", "gy", None),
            P("gx", "gy", None),
            P("gx", "gy", None),
            P("gx", "gy", None),
            P("gy", "gx", None, None),
            P("gx", None, "gy", None),
        ),
        out_specs=(P(None, "gx", "gy", None), P("gx", "gy", None)),
        check_vma=False,
    )
```

profile of v0, /device:TPU:0, one launch (start us, length us, event | category | flops | bytes accessed | tf_op | source)
XLA Modules:
  0.0 75.5 jit_solution(9150187020478586098)
XLA Ops:
  0.6 0.0 copy-start
  0.6 0.0 copy-start.5
  0.7 0.0 copy-start.4
  0.7 0.0 copy-start.8
  0.7 1.4 %fusion.40 = (f32[3,1,16,128]{3,2,1,0:T(8,128)}, f32[3,1,16,128]{3,2,1,0:T(8,128)}) fusion(f32[3,16,16,128]{3,2,1,0:T(8,128)} %param.13), kind=kLoop, calls=%fused_computation.77 | loop fusion | bytes 98304 | tf_op jit(solution)/shard_map/slice | solution.py:13
  2.1 3.0 %collective-permute-start = (f32[3,1,16,128]{3,2,1,0:T(8,128)}, f32[3,1,16,128]{3,2,1,0:T(8,128)}, u32[]{:S(2)}, u32[]{:S(2)}) collective-permute-start(f32[3,1,16,128]{3,2,1,0:T(8,128)} %get-tuple-element.42), channel_id=1, source_target_pairs={{0,2},{2,4},{4,6},{6,8},{8,10},{10,12},{12,14},{14,16},{16,18},{18... | collective-permute-start | bytes 73736 | tf_op jit(solution)/shard_map/ppermute | solution.py:14
  5.1 1.3 %collective-permute-start.1 = (f32[3,1,16,128]{3,2,1,0:T(8,128)}, f32[3,1,16,128]{3,2,1,0:T(8,128)}, u32[]{:S(2)}, u32[]{:S(2)}) collective-permute-start(f32[3,1,16,128]{3,2,1,0:T(8,128)} %get-tuple-element.41), channel_id=1, source_target_pairs={{2,0},{4,2},{6,4},{8,6},{10,8},{12,10},{14,12},{16,14},{18,16},{20... | collective-permute-start | bytes 73736 | tf_op jit(solution)/shard_map/ppermute | solution.py:15
  6.4 1.3 %fusion.39 = (f32[3,16,16,1]{3,2,1,0:T(8,128)S(1)}, f32[3,16,16,1]{3,2,1,0:T(8,128)S(1)}) fusion(f32[3,16,16,128]{3,2,1,0:T(8,128)} %param.13), kind=kLoop, calls=%fused_computation.76 | loop fusion | bytes 12288 | tf_op jit(solution)/shard_map/slice | solution.py:63
  7.7 0.3 copy.61
  8.0 0.4 copy.62
  8.4 0.1 reshape.175
  8.5 0.0 copy-done.5
  8.6 0.0 copy-done.4
  8.6 24.6 %all_gather.3 = bf16[16,1,1536]{2,1,0:T(2,128)(2,1)S(1)} all-gather(bf16[1,1,1536]{2,1,0:T(2,128)(2,1)S(1)} %convert_element_type.8), channel_id=1, replica_groups=mesh['gx'=16,'gy'=2] {'gx'}, dimensions={0}, use_global_device_ids=true | all-gather | bytes 52224 | tf_op jit(solution)/shard_map/all_gather | solution.py:74
  33.2 0.0 copy-done
  33.2 0.0 copy-done.8
  33.2 1.1 %fusion.4 = f32[1,2,1536]{2,0,1:T(1,128)S(1)} fusion(bf16[16,16,1536]{2,1,0:T(8,128)(2,1)S(1)} %bitcast.103, bf16[16,1,1536]{2,1,0:T(2,128)(2,1)S(1)} %all_gather.3, bf16[16,2,1536]{2,1,0:T(2,128)(2,1)S(1)} %bitcast.100), kind=kOutput, calls=%fused_computation.10 | convolution fusion | flops 884752 | bytes 946176 | tf_op jit(solution)/shard_map/rabk,r->abk/dot_general | solution.py:77
  34.4 8.1 %all-reduce.1 = f32[1,2,1536]{2,1,0:T(2,128)S(1)} all-reduce(f32[1,2,1536]{2,1,0:T(2,128)S(1)} %copy.58), channel_id=2, replica_groups=mesh['gx'=16,'gy'=2] {'gy'}, use_global_device_ids=true, to_apply=%region_1.2.clone | all-reduce | flops 3072 | bytes 24576
  42.5 0.0 copy-start.9
  42.5 0.0 copy-start.6
  42.5 0.0 copy-start.7
  42.5 0.0 copy-start.1
  42.5 0.0 copy-start.3
  42.5 8.4 %gather_fusion = f32[1536]{0:T(1024)S(1)} fusion(f32[1536]{0:T(1024)S(1)} %reshape.175, s32[2048]{0:T(1024)S(1)} %pad_clamp_fusion), kind=kCustom, calls=%fused_computation | custom fusion | bytes 18432 | tf_op jit(solution)/shard_map/gather | solution.py:65
  50.9 0.0 copy-start.2
  50.9 0.0 copy-done.9
  50.9 0.7 dynamic-slice.14
  51.6 0.0 copy-done.6
  51.6 0.0 copy-done.7
  51.6 1.3 %fusion.34 = (f32[1,1,1536]{2,1,0:T(1,128)}, f32[1536]{0:T(1024)S(1)}) fusion(f32[1,2,1536]{2,1,0:T(2,128)S(1)} %all-reduce.1, u32[]{:T(128)} %bitcast.32, f32[1,1,1536]{2,1,0:T(1,128)S(1)} %copy-done.6, f32[1536]{0:T(1024)S(1)} %gather_fusion, f32[1,1,1536]{2,1,0:T(1,128)S(1)} %copy-done.7, f32[1,1,1536]{2,1,0:T(1,128)S(1)} %copy-done.4), kind=kLoop, calls=%fused_computation.70 | loop fusion | flops 7680 | bytes 43012 | tf_op jit(solution)/shard_map/add | solution.py:81
  52.9 6.2 %scatter_custom_fusion = f32[1536]{0:T(1024)S(1)} fusion(s32[1536]{0:T(1024)S(1)} %fusion.33, f32[1536]{0:T(1024)S(1)} %get-tuple-element.48, f32[]{:T(128)} %constant.58.clone.1), kind=kCustom, calls=%fused_computation.72 | custom fusion | bytes 6148 | tf_op jit(solution)/shard_map/scatter | solution.py:69
  59.1 0.6 fusion.41
  59.7 0.0 copy-done.1
  59.7 0.1 reshape.170
  59.8 0.8 reshape.171
  60.5 0.0 collective-permute-done
  60.5 0.7 constant_dynamic-update-slice_fusion.6
  61.3 0.1 constant_dynamic-update-slice_fusion.4
  61.4 0.0 collective-permute-done.1
  61.4 0.7 constant_dynamic-update-slice_fusion.3
  62.2 2.4 %collective-permute-start.2 = (f32[3,18,1,128]{3,2,1,0:T(1,128)S(1)}, f32[3,18,1,128]{3,2,1,0:T(1,128)S(1)}, u32[]{:S(2)}, u32[]{:S(2)}) collective-permute-start(f32[3,18,1,128]{3,2,1,0:T(1,128)S(1)} %get-tuple-element.34), channel_id=1, source_target_pairs={{0,1},{2,3},{4,5},{6,7},{8,9},{10,11},{12,13},{14,15},{16,17},{18,... | collective-permute-start | bytes 82952 | tf_op jit(solution)/shard_map/ppermute | solution.py:14
  64.6 1.3 %collective-permute-start.3 = (f32[3,18,1,128]{3,2,1,0:T(1,128)S(1)}, f32[3,18,1,128]{3,2,1,0:T(1,128)S(1)}, u32[]{:S(2)}, u32[]{:S(2)}) collective-permute-start(f32[3,18,1,128]{3,2,1,0:T(1,128)S(1)} %get-tuple-element.35), channel_id=1, source_target_pairs={{1,0},{3,2},{5,4},{7,6},{9,8},{11,10},{13,12},{15,14},{17,16},{19,... | collective-permute-start | bytes 82952 | tf_op jit(solution)/shard_map/ppermute | solution.py:15
  65.9 0.0 copy-done.3
  65.9 0.0 copy-done.2
  65.9 0.2 fusion.12
  66.1 0.0 collective-permute-done.2
  66.1 4.2 %collective-permute-done.3 = f32[3,18,1,128]{3,2,1,0:T(1,128)S(1)} collective-permute-done((f32[3,18,1,128]{3,2,1,0:T(1,128)S(1)}, f32[3,18,1,128]{3,2,1,0:T(1,128)S(1)}, u32[]{:S(2)}, u32[]{:S(2)}) %collective-permute-start.3) | collective-permute-done | bytes 27680 | tf_op jit(solution)/shard_map/ppermute | solution.py:15
  70.4 0.1 pad_maximum_fusion
  70.5 0.2 fusion.8
  70.7 0.1 fusion.14
  70.8 0.8 %pad_maximum_fusion.1 = f32[3,16,16,128]{3,2,1,0:T(8,128)} fusion(f32[1,16,16,128]{3,2,1,0:T(8,128)S(1)} %fusion.14, f32[1,16,16,128]{3,2,1,0:T(8,128)S(1)} %fusion.12, f32[1,16,16,128]{3,2,1,0:T(8,128)S(1)} %fusion.8), kind=kLoop, calls=%fused_computation.12 | loop fusion | flops 196608 | bytes 786432 | tf_op jit(solution)/shard_map/stack | solution.py:36
  71.6 2.1 %copy.51 = f32[3,16,16,128]{2,1,0,3:T(8,128)S(1)} copy(f32[3,16,16,128]{3,2,1,0:T(8,128)} %pad_maximum_fusion.1) | data formatting | bytes 786432 | tf_op jit(solution)/shard_map/stack | solution.py:36
  73.7 1.8 %copy.54 = f32[3,16,16,128]{3,2,1,0:T(8,128)} copy(f32[3,16,16,128]{2,1,0,3:T(8,128)S(1)} %fusion.31) | data formatting | bytes 786432
  (10 shorter events, 0.2 us)
Async XLA Ops:
  0.6 32.6 %copy-start = (bf16[16,1,2,1536]{3,2,1,0:T(2,128)(2,1)S(1)}, bf16[16,1,2,1536]{3,2,1,0:T(2,128)(2,1)}, u32[]{:S(2)}) copy-start(bf16[16,1,2,1536]{3,2,1,0:T(2,128)(2,1)} %param.20) | copy-start | bytes 294916
  0.6 7.9 %copy-start.5 = (s32[1,1,1536]{2,1,0:T(1,128)S(1)}, s32[1,1,1536]{2,1,0:T(1,128)}, u32[]{:S(2)}) copy-start(s32[1,1,1536]{2,1,0:T(1,128)} %param.19) | copy-start | bytes 18436
  0.7 7.9 %copy-start.4 = (f32[1,1,1536]{2,1,0:T(1,128)S(1)}, f32[1,1,1536]{2,1,0:T(1,128)}, u32[]{:S(2)}) copy-start(f32[1,1,1536]{2,1,0:T(1,128)} %param.16) | copy-start | bytes 18436
  0.7 32.6 %copy-start.8 = (bf16[16,16,1,1536]{3,1,2,0:T(8,128)(2,1)S(1)}, bf16[16,16,1,1536]{3,1,2,0:T(8,128)(2,1)}, u32[]{:S(2)}) copy-start(bf16[16,16,1,1536]{3,1,2,0:T(8,128)(2,1)} %param.21) | copy-start | bytes 2359300
  2.1 58.4 %collective-permute-start = (f32[3,1,16,128]{3,2,1,0:T(8,128)}, f32[3,1,16,128]{3,2,1,0:T(8,128)}, u32[]{:S(2)}, u32[]{:S(2)}) collective-permute-start(f32[3,1,16,128]{3,2,1,0:T(8,128)} %get-tuple-element.42), channel_id=1, source_target_pairs={{0,2},{2,4},{4,6},{6,8},{8,10},{10,12},{12,14},{14,16},{16,18},{18... | collective-permute-start | bytes 73736 | tf_op jit(solution)/shard_map/ppermute | solution.py:14
  5.1 56.3 %collective-permute-start.1 = (f32[3,1,16,128]{3,2,1,0:T(8,128)}, f32[3,1,16,128]{3,2,1,0:T(8,128)}, u32[]{:S(2)}, u32[]{:S(2)}) collective-permute-start(f32[3,1,16,128]{3,2,1,0:T(8,128)} %get-tuple-element.41), channel_id=1, source_target_pairs={{2,0},{4,2},{6,4},{8,6},{10,8},{12,10},{14,12},{16,14},{18,16},{20... | collective-permute-start | bytes 73736 | tf_op jit(solution)/shard_map/ppermute | solution.py:15
  42.5 8.5 %copy-start.9 = (u32[32]{0:T(128)S(1)}, u32[32]{0:T(128)}, u32[]{:S(2)}) copy-start(u32[32]{0:T(128)} %constant.72) | copy-start | bytes 388
  42.5 9.1 %copy-start.6 = (f32[1,1,1536]{2,1,0:T(1,128)S(1)}, f32[1,1,1536]{2,1,0:T(1,128)}, u32[]{:S(2)}) copy-start(f32[1,1,1536]{2,1,0:T(1,128)} %param.18) | copy-start | bytes 18436
  42.5 9.1 %copy-start.7 = (f32[1,1,1536]{2,1,0:T(1,128)S(1)}, f32[1,1,1536]{2,1,0:T(1,128)}, u32[]{:S(2)}) copy-start(f32[1,1,1536]{2,1,0:T(1,128)} %param.17) | copy-start | bytes 18436
  42.5 17.2 %copy-start.1 = (f32[3,16,16,128]{3,2,1,0:T(8,128)S(1)}, f32[3,16,16,128]{3,2,1,0:T(8,128)}, u32[]{:S(2)}) copy-start(f32[3,16,16,128]{3,2,1,0:T(8,128)} %param.13) | copy-start | bytes 1179652
  42.5 23.4 %copy-start.3 = (f32[3,3,16,16,128]{4,3,2,1,0:T(8,128)S(1)}, f32[3,3,16,16,128]{4,3,2,1,0:T(8,128)}, u32[]{:S(2)}) copy-start(f32[3,3,16,16,128]{4,3,2,1,0:T(8,128)} %param.14) | copy-start | bytes 3538948
  50.9 15.0 %copy-start.2 = (f32[6,2,16,16,128]{4,3,2,1,0:T(8,128)S(1)}, f32[6,2,16,16,128]{4,3,2,1,0:T(8,128)}, u32[]{:S(2)}) copy-start(f32[6,2,16,16,128]{4,3,2,1,0:T(8,128)} %param.15) | copy-start | bytes 4718596
  62.2 4.0 %collective-permute-start.2 = (f32[3,18,1,128]{3,2,1,0:T(1,128)S(1)}, f32[3,18,1,128]{3,2,1,0:T(1,128)S(1)}, u32[]{:S(2)}, u32[]{:S(2)}) collective-permute-start(f32[3,18,1,128]{3,2,1,0:T(1,128)S(1)} %get-tuple-element.34), channel_id=1, source_target_pairs={{0,1},{2,3},{4,5},{6,7},{8,9},{10,11},{12,13},{14,15},{16,17},{18,... | collective-permute-start | bytes 82952 | tf_op jit(solution)/shard_map/ppermute | solution.py:14
  64.6 5.8 %collective-permute-start.3 = (f32[3,18,1,128]{3,2,1,0:T(1,128)S(1)}, f32[3,18,1,128]{3,2,1,0:T(1,128)S(1)}, u32[]{:S(2)}, u32[]{:S(2)}) collective-permute-start(f32[3,18,1,128]{3,2,1,0:T(1,128)S(1)} %get-tuple-element.35), channel_id=1, source_target_pairs={{1,0},{3,2},{5,4},{7,6},{9,8},{11,10},{13,12},{15,14},{17,16},{19,... | collective-permute-start | bytes 82952 | tf_op jit(solution)/shard_map/ppermute | solution.py:15
where the time goes:
time: 75.9 us; the launch traced here: 75.5 us
  blocking collectives  32.7 us (43%)
  local copies, waits for them, and re-layouts  25.7 us (34%)
  starting transfers between devices  7.98 us (11%)
  waiting for transfers between devices  4.27 us (6%)
  other arithmetic  2.72 us (4%)
  matrix products  1.12 us (1%)
  between operations  0.9 us (1%)
    all_gather x1, blocking collectives, on_device(): gathered = lax.all_gather(boundary_half, 'gx', axis=0, tiled=True)  24.6 us
    gather x1, local copies, waits for them, and re-layouts, on_device(): edge_trace = surface[owner_flat].reshape(boundary_field.shape)  8.39 us
    unnamed x1, blocking collectives  8.11 us
    scatter x1, local copies, waits for them, and re-layouts, on_device(): placed = jnp.zeros((boundary_count,), jnp.float32).at[owner_flat].set((co...  6.18 us
    ppermute x2, starting transfers between devices, with_halo(): before = lax.ppermute(last, axis, up)  5.41 us
    ppermute x2, waiting for transfers between devices, with_halo(): after = lax.ppermute(initial, axis, down)  4.23 us
    unnamed x26, local copies, waits for them, and re-layouts  4.02 us
    ppermute x2, starting transfers between devices, with_halo(): after = lax.ppermute(initial, axis, down)  2.57 us
  transfers between devices with their start and end apart: 4, of which 1 were waited for; matrix products, arithmetic and copies ran while one was open for 29% of the time, Pallas kernels for 0%

commit v1 on v0

--- a/solution.py
+++ b/solution.py
@@ -71,7 +71,12 @@
     placed = placed.reshape(2, 3, cells_x, cells_y)
     volume_out = stiffness.at[:, :, :, 0].add(placed[0]).at[:, :, :, -1].add(placed[1])
     boundary_half = boundary_field.astype(jnp.bfloat16)
-    gathered = lax.all_gather(boundary_half, "gx", axis=0, tiled=True)
+    ring = [boundary_half]
+    for hop in range(15):
+        ring.append(lax.ppermute(ring[-1], "gx", [(dev, (dev + 1) % 16) for dev in range(16)]))
+    gathered = jnp.roll(
+        jnp.concatenate(ring[::-1], axis=0), (lax.axis_index("gx") + 1) * ring[0].shape[0], axis=0
+    )
     coef = jnp.einsum("rxbk,xbk->r", right_basis, gathered, preferred_element_type=jnp.float32)
     coef_half = coef.astype(jnp.bfloat16)
     partial_value = jnp.einsum(

time: 75.9 us -> 125 us (1.65)
  waiting for transfers between devices: 4.27 us -> 67 us
  blocking collectives: 32.7 us -> 9.76 us
  other arithmetic: 2.72 us -> 9.84 us
    ppermute x0 -> x15, waiting for transfers between devices: none -> 67 us  [on_device(): lax.ppermute(ring[-1], 'gx', [(dev, (dev + 1) % 16) for dev in range(16)])]
    all_gather x1 -> x0, blocking collectives: 24.6 us -> none  [on_device(): gathered = lax.all_gather(boundary_half, 'gx', axis=0, tiled=True)]
    ppermute x2, waiting for transfers between devices: 4.23 us -> 0.01 us  [with_halo(): after = lax.ppermute(initial, axis, down)]
    scatter-add x2, other arithmetic: 0.01 us -> 2.69 us  [on_device(): stiffness.at[:, :, :, 0].add(placed[0]).at[:, :, :, -1].add(placed[1])]
    sub x3, other arithmetic: 0.46 us -> 3.03 us  [apply_blocks(): comp_rows[tangent[slot]]]
    unnamed x26 -> x82, local copies, waits for them, and re-layouts: 4.02 us -> 5.79 us
    unnamed x1, blocking collectives: 8.11 us -> 9.76 us
  transfers between devices with their start and end apart: 4 -> 19, of which waited for: 1 -> 13; matrix products, arithmetic and copies ran while one was open for 29% -> 21% of each run, Pallas kernels for 0% -> 0%
where the time goes in v1:
time: 125 us
  waiting for transfers between devices  67 us (54%)
  local copies, waits for them, and re-layouts  25.8 us (21%)
  other arithmetic  9.84 us (8%)
  blocking collectives  9.76 us (8%)
  starting transfers between devices  8.98 us (7%)
  matrix products  2.16 us (2%)
    ppermute x15, waiting for transfers between devices, on_device(): lax.ppermute(ring[-1], 'gx', [(dev, (dev + 1) % 16) for dev in range(16)])  67 us
    unnamed x1, blocking collectives  9.76 us
    gather x1, local copies, waits for them, and re-layouts, on_device(): edge_trace = surface[owner_flat].reshape(boundary_field.shape)  8.39 us
    scatter x1, local copies, waits for them, and re-layouts, on_device(): placed = jnp.zeros((boundary_count,), jnp.float32).at[owner_flat].set((co...  6.18 us
    unnamed x82, local copies, waits for them, and re-layouts  5.79 us
    ppermute x2, starting transfers between devices, with_halo(): before = lax.ppermute(last, axis, up)  5.77 us
    sub x3, other arithmetic, apply_blocks(): comp_rows[tangent[slot]]  3.03 us
    scatter-add x2, other arithmetic, on_device(): stiffness.at[:, :, :, 0].add(placed[0]).at[:, :, :, -1].add(placed[1])  2.69 us
  transfers between devices with their start and end apart: 19, of which 13 were waited for; matrix products, arithmetic and copies ran while one was open for 21% of the time, Pallas kernels for 0%

profile of v1, /device:TPU:0, one launch (start us, length us, event | category | flops | bytes accessed | tf_op | source)
XLA Modules:
  0.0 124.8 jit_solution(4269798558740508668)
XLA Ops:
  0.6 0.0 copy-start
  0.6 0.0 copy-start.1
  0.7 0.8 convert_element_type.8
  1.5 0.5 collective-permute-start.4
  2.0 6.3 %collective-permute-done.4 = bf16[1,1,1536]{2,1,0:T(2,128)(2,1)S(1)} collective-permute-done((bf16[1,1,1536]{2,1,0:T(2,128)(2,1)S(1)}, bf16[1,1,1536]{2,1,0:T(2,128)(2,1)S(1)}, u32[]{:S(2)}, u32[]{:S(2)}) %collective-permute-start.4) | collective-permute-done | bytes 3104 | tf_op jit(solution)/shard_map/ppermute | solution.py:76
  8.2 0.0 collective-permute-start.5
  8.2 5.7 %collective-permute-done.5 = bf16[1,1,1536]{2,1,0:T(2,128)(2,1)S(1)} collective-permute-done((bf16[1,1,1536]{2,1,0:T(2,128)(2,1)S(1)}, bf16[1,1,1536]{2,1,0:T(2,128)(2,1)S(1)}, u32[]{:S(2)}, u32[]{:S(2)}) %collective-permute-start.5) | collective-permute-done | bytes 3104 | tf_op jit(solution)/shard_map/ppermute | solution.py:76
  14.0 0.0 collective-permute-start.6
  14.0 5.7 %collective-permute-done.6 = bf16[1,1,1536]{2,1,0:T(2,128)(2,1)S(1)} collective-permute-done((bf16[1,1,1536]{2,1,0:T(2,128)(2,1)S(1)}, bf16[1,1,1536]{2,1,0:T(2,128)(2,1)S(1)}, u32[]{:S(2)}, u32[]{:S(2)}) %collective-permute-start.6) | collective-permute-done | bytes 3104 | tf_op jit(solution)/shard_map/ppermute | solution.py:76
  19.7 0.0 collective-permute-start.7
  19.7 5.7 %collective-permute-done.7 = bf16[1,1,1536]{2,1,0:T(2,128)(2,1)S(1)} collective-permute-done((bf16[1,1,1536]{2,1,0:T(2,128)(2,1)S(1)}, bf16[1,1,1536]{2,1,0:T(2,128)(2,1)S(1)}, u32[]{:S(2)}, u32[]{:S(2)}) %collective-permute-start.7) | collective-permute-done | bytes 3104 | tf_op jit(solution)/shard_map/ppermute | solution.py:76
  25.5 0.0 collective-permute-start.8
  25.5 5.7 %collective-permute-done.8 = bf16[1,1,1536]{2,1,0:T(2,128)(2,1)S(1)} collective-permute-done((bf16[1,1,1536]{2,1,0:T(2,128)(2,1)S(1)}, bf16[1,1,1536]{2,1,0:T(2,128)(2,1)S(1)}, u32[]{:S(2)}, u32[]{:S(2)}) %collective-permute-start.8) | collective-permute-done | bytes 3104 | tf_op jit(solution)/shard_map/ppermute | solution.py:76
  31.2 0.0 collective-permute-start.9
  31.2 0.8 fusion.44
  32.0 1.3 %collective-permute-start = (f32[3,1,16,128]{3,2,1,0:T(8,128)S(1)}, f32[3,1,16,128]{3,2,1,0:T(8,128)S(1)}, u32[]{:S(2)}, u32[]{:S(2)}) collective-permute-start(f32[3,1,16,128]{3,2,1,0:T(8,128)S(1)} %get-tuple-element.40), channel_id=1, source_target_pairs={{0,2},{2,4},{4,6},{6,8},{8,10},{10,12},{12,14},{14,16},{16,18},{18... | collective-permute-start | bytes 73736 | tf_op jit(solution)/shard_map/ppermute | solution.py:14
  33.3 1.3 %collective-permute-start.1 = (f32[3,1,16,128]{3,2,1,0:T(8,128)S(1)}, f32[3,1,16,128]{3,2,1,0:T(8,128)}, u32[]{:S(2)}, u32[]{:S(2)}) collective-permute-start(f32[3,1,16,128]{3,2,1,0:T(8,128)S(1)} %get-tuple-element.39), channel_id=1, source_target_pairs={{2,0},{4,2},{6,4},{8,6},{10,8},{12,10},{14,12},{16,14},{18,16},{20... | collective-permute-start | bytes 73736 | tf_op jit(solution)/shard_map/ppermute | solution.py:15
  34.6 2.4 %collective-permute-done.9 = bf16[1,1,1536]{2,1,0:T(2,128)(2,1)S(1)} collective-permute-done((bf16[1,1,1536]{2,1,0:T(2,128)(2,1)S(1)}, bf16[1,1,1536]{2,1,0:T(2,128)(2,1)S(1)}, u32[]{:S(2)}, u32[]{:S(2)}) %collective-permute-start.9) | collective-permute-done | bytes 3104 | tf_op jit(solution)/shard_map/ppermute | solution.py:76
  37.0 0.0 collective-permute-start.10
  37.0 1.4 %fusion.43 = (f32[3,16,16,1]{3,2,1,0:T(8,128)S(1)}, f32[3,16,16,1]{3,2,1,0:T(8,128)S(1)}) fusion(f32[3,16,16,128]{3,2,1,0:T(8,128)} %param.13), kind=kLoop, calls=%fused_computation.110 | loop fusion | bytes 12288 | tf_op jit(solution)/shard_map/slice | solution.py:63
  38.4 4.4 %collective-permute-done.10 = bf16[1,1,1536]{2,1,0:T(2,128)(2,1)S(1)} collective-permute-done((bf16[1,1,1536]{2,1,0:T(2,128)(2,1)S(1)}, bf16[1,1,1536]{2,1,0:T(2,128)(2,1)S(1)}, u32[]{:S(2)}, u32[]{:S(2)}) %collective-permute-start.10) | collective-permute-done | bytes 3104 | tf_op jit(solution)/shard_map/ppermute | solution.py:76
  42.7 0.1 collective-permute-start.11
  42.8 0.3 copy.56
  43.2 0.4 copy.57
  43.5 5.0 %collective-permute-done.11 = bf16[1,1,1536]{2,1,0:T(2,128)(2,1)S(1)} collective-permute-done((bf16[1,1,1536]{2,1,0:T(2,128)(2,1)S(1)}, bf16[1,1,1536]{2,1,0:T(2,128)(2,1)S(1)}, u32[]{:S(2)}, u32[]{:S(2)}) %collective-permute-start.11) | collective-permute-done | bytes 3104 | tf_op jit(solution)/shard_map/ppermute | solution.py:76
  48.5 0.0 collective-permute-start.12
  48.6 5.7 %collective-permute-done.12 = bf16[1,1,1536]{2,1,0:T(2,128)(2,1)S(1)} collective-permute-done((bf16[1,1,1536]{2,1,0:T(2,128)(2,1)S(1)}, bf16[1,1,1536]{2,1,0:T(2,128)(2,1)S(1)}, u32[]{:S(2)}, u32[]{:S(2)}) %collective-permute-start.12) | collective-permute-done | bytes 3104 | tf_op jit(solution)/shard_map/ppermute | solution.py:76
  54.3 0.0 collective-permute-start.13
  54.4 0.1 reshape.175
  54.5 8.4 %gather_fusion = f32[1536]{0:T(1024)S(1)} fusion(f32[1536]{0:T(1024)S(1)} %reshape.175, s32[2048]{0:T(1024)S(1)} %pad_clamp_fusion), kind=kCustom, calls=%fused_computation | custom fusion | bytes 18432 | tf_op jit(solution)/shard_map/gather | solution.py:65
  62.9 0.0 copy-start.2
  62.9 0.7 dynamic-slice.14
  63.6 0.0 collective-permute-start.14
  63.6 0.0 collective-permute-done
  63.6 5.7 %collective-permute-done.14 = bf16[1,1,1536]{2,1,0:T(2,128)(2,1)S(1)} collective-permute-done((bf16[1,1,1536]{2,1,0:T(2,128)(2,1)S(1)}, bf16[1,1,1536]{2,1,0:T(2,128)(2,1)S(1)}, u32[]{:S(2)}, u32[]{:S(2)}) %collective-permute-start.14) | collective-permute-done | bytes 3104 | tf_op jit(solution)/shard_map/ppermute | solution.py:76
  69.4 0.0 copy-start.7
  69.4 0.1 constant_dynamic-update-slice_fusion.4
  69.5 5.6 %collective-permute-done.15 = bf16[1,1,1536]{2,1,0:T(2,128)(2,1)S(1)} collective-permute-done((bf16[1,1,1536]{2,1,0:T(2,128)(2,1)S(1)}, bf16[1,1,1536]{2,1,0:T(2,128)(2,1)S(1)}, u32[]{:S(2)}, u32[]{:S(2)}) %collective-permute-start.15) | collective-permute-done | bytes 3104 | tf_op jit(solution)/shard_map/ppermute | solution.py:76
  75.1 0.7 constant_dynamic-update-slice_fusion.3
  75.9 5.0 %collective-permute-done.16 = bf16[1,1,1536]{2,1,0:T(2,128)(2,1)S(1)} collective-permute-done((bf16[1,1,1536]{2,1,0:T(2,128)(2,1)S(1)}, bf16[1,1,1536]{2,1,0:T(2,128)(2,1)S(1)}, u32[]{:S(2)}, u32[]{:S(2)}) %collective-permute-start.16) | collective-permute-done | bytes 3104 | tf_op jit(solution)/shard_map/ppermute | solution.py:76
  80.9 0.0 collective-permute-start.17
  80.9 0.0 copy-start.19
  80.9 4.5 %collective-permute-start.2 = (f32[3,18,1,128]{3,2,1,0:T(1,128)S(1)}, f32[3,18,1,128]{3,2,1,0:T(1,128)}, u32[]{:S(2)}, u32[]{:S(2)}) collective-permute-start(f32[3,18,1,128]{3,2,1,0:T(1,128)S(1)} %get-tuple-element.32), channel_id=1, source_target_pairs={{0,1},{2,3},{4,5},{6,7},{8,9},{10,11},{12,13},{14,15},{16,17},{18,... | collective-permute-start | bytes 82952 | tf_op jit(solution)/shard_map/ppermute | solution.py:14
  85.4 1.3 %collective-permute-start.3 = (f32[3,18,1,128]{3,2,1,0:T(1,128)S(1)}, f32[3,18,1,128]{3,2,1,0:T(1,128)}, u32[]{:S(2)}, u32[]{:S(2)}) collective-permute-start(f32[3,18,1,128]{3,2,1,0:T(1,128)S(1)} %get-tuple-element.33), channel_id=1, source_target_pairs={{1,0},{3,2},{5,4},{7,6},{9,8},{11,10},{13,12},{15,14},{17,16},{19,... | collective-permute-start | bytes 82952 | tf_op jit(solution)/shard_map/ppermute | solution.py:15
  86.7 0.1 collective-permute-start.18
  86.8 1.8 %fusion.12 = f32[1,16,16,128]{3,2,1,0:T(8,128)} fusion(f32[2,16,16,128]{3,2,1,0:T(8,128)S(1)} %slice.250, f32[3,17,16,128]{3,2,1,0:T(8,128)S(1)} %get-tuple-element.38, f32[3,17,16,128]{3,2,1,0:T(8,128)S(1)} %get-tuple-element.41, f32[6,2,16,16,128]{4,3,2,1,0:T(8,128)S(1)} %copy-done.2, f32[3,3,16,16,128]{4,3,2,1,0:T(8,128)} %param.14, ...), kind=kLoop, calls=%fused_computation.19 | loop fusion | flops 425984 | bytes 1966080 | tf_op jit(solution)/shard_map/sub | solution.py:34
  88.6 3.9 %collective-permute-done.18 = bf16[1,1,1536]{2,1,0:T(2,128)(2,1)S(1)} collective-permute-done((bf16[1,1,1536]{2,1,0:T(2,128)(2,1)S(1)}, bf16[1,1,1536]{2,1,0:T(2,128)(2,1)S(1)}, u32[]{:S(2)}, u32[]{:S(2)}) %collective-permute-start.18) | collective-permute-done | bytes 3104 | tf_op jit(solution)/shard_map/ppermute | solution.py:76
  93.2 0.0 copy-start.21
  93.2 0.7 copy-done.21
  93.9 2.2 %fusion.4 = f32[1,2,1536]{2,0,1:T(1,128)S(1)} fusion(bf16[16,16,1536]{2,1,0:T(8,128)(2,1)S(1)} %bitcast.100, bf16[16,2,1536]{2,1,0:T(2,128)(2,1)} %bitcast.103, bf16[32,1,1536]{2,1,0:T(2,128)(2,1)} %copy-done.21, s32[]{:T(128)S(6)} %select_n.26), kind=kOutput, calls=%fused_computation.10 | convolution fusion | flops 884752 | bytes 995332 | tf_op jit(solution)/shard_map/rabk,r->abk/dot_general | solution.py:82
  96.1 9.8 %all-reduce.1 = f32[1,2,1536]{2,1,0:T(2,128)S(1)} all-reduce(f32[1,2,1536]{2,1,0:T(2,128)S(1)} %copy.53), channel_id=2, replica_groups=mesh['gx'=16,'gy'=2] {'gy'}, use_global_device_ids=true, to_apply=%region_1.2.clone | all-reduce | flops 3072 | bytes 24576
  105.8 2.0 %fusion.36 = (f32[1,1,1536]{2,1,0:T(1,128)}, f32[1536]{0:T(1024)S(1)}) fusion(f32[1,2,1536]{2,1,0:T(2,128)S(1)} %all-reduce.1, u32[]{:T(128)} %bitcast.32, f32[1,1,1536]{2,1,0:T(1,128)} %param.18, f32[1536]{0:T(1024)S(1)} %gather_fusion, f32[1,1,1536]{2,1,0:T(1,128)} %param.17, f32[1,1,1536]{2,1,0:T(1,128)S(1)} %copy-done.7), kind=kLoop, calls=%fused_computation.103 | loop fusion | flops 7680 | bytes 43012 | tf_op jit(solution)/shard_map/add | solution.py:86
  107.8 6.2 %scatter_custom_fusion = f32[1536]{0:T(1024)S(1)} fusion(s32[1536]{0:T(1024)S(1)} %fusion.35, f32[1536]{0:T(1024)S(1)} %get-tuple-element.46, f32[]{:T(128)} %constant.81.clone.1), kind=kCustom, calls=%fused_computation.105 | custom fusion | bytes 6148 | tf_op jit(solution)/shard_map/scatter | solution.py:69
  114.0 0.1 reshape.170
  114.1 0.1 reshape.171
  114.2 0.0 collective-permute-done.2
  114.2 1.2 pad_maximum_fusion
  115.5 0.1 copy-done.3
  115.6 1.1 fusion.14
  116.7 0.2 fusion.8
  116.9 2.2 %copy.46 = f32[3,16,16,128]{2,1,0,3:T(8,128)} copy(f32[3,16,16,128]{3,2,1,0:T(8,128)S(1)} %pad_maximum_fusion.1) | data formatting | bytes 786432 | tf_op jit(solution)/shard_map/stack | solution.py:36
  119.1 1.3 %fusion.34 = f32[3,16,16,128]{2,1,0,3:T(8,128)} fusion(f32[3,16,16,128]{2,1,0,3:T(8,128)} %copy.46, f32[3,16,16,1]{2,1,0,3:T(8,128)S(1)} %reshape.170), kind=kLoop, calls=%fused_computation.99 | loop fusion | flops 768 | bytes 52224 | tf_op jit(solution)/shard_map/scatter-add | solution.py:72
  120.4 1.3 %fusion.33 = f32[3,16,16,128]{2,1,0,3:T(8,128)} fusion(f32[3,16,16,128]{2,1,0,3:T(8,128)} %fusion.34, f32[3,16,16,1]{2,1,0,3:T(8,128)S(1)} %reshape.171), kind=kLoop, calls=%fused_computation.97 | loop fusion | flops 768 | bytes 52224 | tf_op jit(solution)/shard_map/scatter-add | solution.py:72
  121.8 3.0 %copy.49 = f32[3,16,16,128]{3,2,1,0:T(8,128)} copy(f32[3,16,16,128]{2,1,0,3:T(8,128)} %fusion.33) | data formatting | bytes 786432
  (86 shorter events, 0.7 us)
Async XLA Ops:
  0.6 92.6 %copy-start = (bf16[16,16,1,1536]{3,1,2,0:T(8,128)(2,1)S(1)}, bf16[16,16,1,1536]{3,1,2,0:T(8,128)(2,1)}, u32[]{:S(2)}) copy-start(bf16[16,16,1,1536]{3,1,2,0:T(8,128)(2,1)} %param.21) | copy-start | bytes 2359300
  0.6 53.7 %copy-start.1 = (f32[3,16,16,128]{3,2,1,0:T(8,128)S(1)}, f32[3,16,16,128]{3,2,1,0:T(8,128)}, u32[]{:S(2)}) copy-start(f32[3,16,16,128]{3,2,1,0:T(8,128)} %param.13) | copy-start | bytes 1179652
  0.7 42.1 %copy-start.20 = (s32[1,1,1536]{2,1,0:T(1,128)S(1)}, s32[1,1,1536]{2,1,0:T(1,128)}, u32[]{:S(2)}) copy-start(s32[1,1,1536]{2,1,0:T(1,128)} %param.19) | copy-start | bytes 18436
  1.5 6.8 %collective-permute-start.4 = (bf16[1,1,1536]{2,1,0:T(2,128)(2,1)S(1)}, bf16[1,1,1536]{2,1,0:T(2,128)(2,1)S(1)}, u32[]{:S(2)}, u32[]{:S(2)}) collective-permute-start(bf16[1,1,1536]{2,1,0:T(2,128)(2,1)S(1)} %convert_element_type.8), channel_id=1, source_target_pairs={{0,2},{2,4},{4,6},{6,8},{8,10},{10,12},{12,14},{14,16},{16,18},{18... | collective-permute-start | bytes 9224 | tf_op jit(solution)/shard_map/ppermute | solution.py:76
  8.2 5.8 %collective-permute-start.5 = (bf16[1,1,1536]{2,1,0:T(2,128)(2,1)S(1)}, bf16[1,1,1536]{2,1,0:T(2,128)(2,1)S(1)}, u32[]{:S(2)}, u32[]{:S(2)}) collective-permute-start(bf16[1,1,1536]{2,1,0:T(2,128)(2,1)S(1)} %collective-permute-done.4), channel_id=1, source_target_pairs={{0,2},{2,4},{4,6},{6,8},{8,10},{10,12},{12,14},{14,16},{16,18},{18... | collective-permute-start | bytes 9224 | tf_op jit(solution)/shard_map/ppermute | solution.py:76
  14.0 5.8 %collective-permute-start.6 = (bf16[1,1,1536]{2,1,0:T(2,128)(2,1)S(1)}, bf16[1,1,1536]{2,1,0:T(2,128)(2,1)S(1)}, u32[]{:S(2)}, u32[]{:S(2)}) collective-permute-start(bf16[1,1,1536]{2,1,0:T(2,128)(2,1)S(1)} %collective-permute-done.5), channel_id=1, source_target_pairs={{0,2},{2,4},{4,6},{6,8},{8,10},{10,12},{12,14},{14,16},{16,18},{18... | collective-permute-start | bytes 9224 | tf_op jit(solution)/shard_map/ppermute | solution.py:76
  19.7 5.8 %collective-permute-start.7 = (bf16[1,1,1536]{2,1,0:T(2,128)(2,1)S(1)}, bf16[1,1,1536]{2,1,0:T(2,128)(2,1)S(1)}, u32[]{:S(2)}, u32[]{:S(2)}) collective-permute-start(bf16[1,1,1536]{2,1,0:T(2,128)(2,1)S(1)} %collective-permute-done.6), channel_id=1, source_target_pairs={{0,2},{2,4},{4,6},{6,8},{8,10},{10,12},{12,14},{14,16},{16,18},{18... | collective-permute-start | bytes 9224 | tf_op jit(solution)/shard_map/ppermute | solution.py:76
  25.5 5.8 %collective-permute-start.8 = (bf16[1,1,1536]{2,1,0:T(2,128)(2,1)S(1)}, bf16[1,1,1536]{2,1,0:T(2,128)(2,1)S(1)}, u32[]{:S(2)}, u32[]{:S(2)}) collective-permute-start(bf16[1,1,1536]{2,1,0:T(2,128)(2,1)S(1)} %collective-permute-done.7), channel_id=1, source_target_pairs={{0,2},{2,4},{4,6},{6,8},{8,10},{10,12},{12,14},{14,16},{16,18},{18... | collective-permute-start | bytes 9224 | tf_op jit(solution)/shard_map/ppermute | solution.py:76
  31.2 11.5 %copy-start.8 = (bf16[1,1,1536]{2,1,0:T(2,128)(2,1)}, bf16[1,1,1536]{2,1,0:T(2,128)(2,1)S(1)}, u32[]{:S(2)}) copy-start(bf16[1,1,1536]{2,1,0:T(2,128)(2,1)S(1)} %collective-permute-done.8) | copy-start | bytes 9220
  31.2 5.8 %collective-permute-start.9 = (bf16[1,1,1536]{2,1,0:T(2,128)(2,1)S(1)}, bf16[1,1,1536]{2,1,0:T(2,128)(2,1)S(1)}, u32[]{:S(2)}, u32[]{:S(2)}) collective-permute-start(bf16[1,1,1536]{2,1,0:T(2,128)(2,1)S(1)} %collective-permute-done.8), channel_id=1, source_target_pairs={{0,2},{2,4},{4,6},{6,8},{8,10},{10,12},{12,14},{14,16},{16,18},{18... | collective-permute-start | bytes 9224 | tf_op jit(solution)/shard_map/ppermute | solution.py:76
  32.0 31.6 %collective-permute-start = (f32[3,1,16,128]{3,2,1,0:T(8,128)S(1)}, f32[3,1,16,128]{3,2,1,0:T(8,128)S(1)}, u32[]{:S(2)}, u32[]{:S(2)}) collective-permute-start(f32[3,1,16,128]{3,2,1,0:T(8,128)S(1)} %get-tuple-element.40), channel_id=1, source_target_pairs={{0,2},{2,4},{4,6},{6,8},{8,10},{10,12},{12,14},{14,16},{16,18},{18... | collective-permute-start | bytes 73736 | tf_op jit(solution)/shard_map/ppermute | solution.py:14
  33.3 41.8 %collective-permute-start.1 = (f32[3,1,16,128]{3,2,1,0:T(8,128)S(1)}, f32[3,1,16,128]{3,2,1,0:T(8,128)}, u32[]{:S(2)}, u32[]{:S(2)}) collective-permute-start(f32[3,1,16,128]{3,2,1,0:T(8,128)S(1)} %get-tuple-element.39), channel_id=1, source_target_pairs={{2,0},{4,2},{6,4},{8,6},{10,8},{12,10},{14,12},{16,14},{18,16},{20... | collective-permute-start | bytes 73736 | tf_op jit(solution)/shard_map/ppermute | solution.py:15
  37.0 5.8 %copy-start.10 = (bf16[1,1,1536]{2,1,0:T(2,128)(2,1)}, bf16[1,1,1536]{2,1,0:T(2,128)(2,1)S(1)}, u32[]{:S(2)}) copy-start(bf16[1,1,1536]{2,1,0:T(2,128)(2,1)S(1)} %collective-permute-done.9) | copy-start | bytes 9220
  37.0 5.8 %collective-permute-start.10 = (bf16[1,1,1536]{2,1,0:T(2,128)(2,1)S(1)}, bf16[1,1,1536]{2,1,0:T(2,128)(2,1)S(1)}, u32[]{:S(2)}, u32[]{:S(2)}) collective-permute-start(bf16[1,1,1536]{2,1,0:T(2,128)(2,1)S(1)} %collective-permute-done.9), channel_id=1, source_target_pairs={{0,2},{2,4},{4,6},{6,8},{8,10},{10,12},{12,14},{14,16},{16,18},{18... | collective-permute-start | bytes 9224 | tf_op jit(solution)/shard_map/ppermute | solution.py:76
  42.7 20.1 %copy-start.12 = (bf16[1,1,1536]{2,1,0:T(2,128)(2,1)}, bf16[1,1,1536]{2,1,0:T(2,128)(2,1)S(1)}, u32[]{:S(2)}) copy-start(bf16[1,1,1536]{2,1,0:T(2,128)(2,1)S(1)} %collective-permute-done.10) | copy-start | bytes 9220
  42.7 5.8 %collective-permute-start.11 = (bf16[1,1,1536]{2,1,0:T(2,128)(2,1)S(1)}, bf16[1,1,1536]{2,1,0:T(2,128)(2,1)S(1)}, u32[]{:S(2)}, u32[]{:S(2)}) collective-permute-start(bf16[1,1,1536]{2,1,0:T(2,128)(2,1)S(1)} %collective-permute-done.10), channel_id=1, source_target_pairs={{0,2},{2,4},{4,6},{6,8},{8,10},{10,12},{12,14},{14,16},{16,18},{18... | collective-permute-start | bytes 9224 | tf_op jit(solution)/shard_map/ppermute | solution.py:76
  48.5 14.3 %copy-start.14 = (bf16[1,1,1536]{2,1,0:T(2,128)(2,1)}, bf16[1,1,1536]{2,1,0:T(2,128)(2,1)S(1)}, u32[]{:S(2)}) copy-start(bf16[1,1,1536]{2,1,0:T(2,128)(2,1)S(1)} %collective-permute-done.11) | copy-start | bytes 9220
  48.5 5.8 %collective-permute-start.12 = (bf16[1,1,1536]{2,1,0:T(2,128)(2,1)S(1)}, bf16[1,1,1536]{2,1,0:T(2,128)(2,1)S(1)}, u32[]{:S(2)}, u32[]{:S(2)}) collective-permute-start(bf16[1,1,1536]{2,1,0:T(2,128)(2,1)S(1)} %collective-permute-done.11), channel_id=1, source_target_pairs={{0,2},{2,4},{4,6},{6,8},{8,10},{10,12},{12,14},{14,16},{16,18},{18... | collective-permute-start | bytes 9224 | tf_op jit(solution)/shard_map/ppermute | solution.py:76
  54.3 8.6 %copy-start.16 = (bf16[1,1,1536]{2,1,0:T(2,128)(2,1)}, bf16[1,1,1536]{2,1,0:T(2,128)(2,1)S(1)}, u32[]{:S(2)}) copy-start(bf16[1,1,1536]{2,1,0:T(2,128)(2,1)S(1)} %collective-permute-done.12) | copy-start | bytes 9220
  54.3 9.3 %collective-permute-start.13 = (bf16[1,1,1536]{2,1,0:T(2,128)(2,1)S(1)}, bf16[1,1,1536]{2,1,0:T(2,128)(2,1)S(1)}, u32[]{:S(2)}, u32[]{:S(2)}) collective-permute-start(bf16[1,1,1536]{2,1,0:T(2,128)(2,1)S(1)} %collective-permute-done.12), channel_id=1, source_target_pairs={{0,2},{2,4},{4,6},{6,8},{8,10},{10,12},{12,14},{14,16},{16,18},{18... | collective-permute-start | bytes 9224 | tf_op jit(solution)/shard_map/ppermute | solution.py:76
  54.5 8.5 %copy-start.22 = (u32[32]{0:T(128)S(1)}, u32[32]{0:T(128)}, u32[]{:S(2)}) copy-start(u32[32]{0:T(128)} %constant.101) | copy-start | bytes 388
  62.9 23.9 %copy-start.2 = (f32[6,2,16,16,128]{4,3,2,1,0:T(8,128)S(1)}, f32[6,2,16,16,128]{4,3,2,1,0:T(8,128)}, u32[]{:S(2)}) copy-start(f32[6,2,16,16,128]{4,3,2,1,0:T(8,128)} %param.15) | copy-start | bytes 4718596
  63.6 17.3 %copy-start.18 = (bf16[1,1,1536]{2,1,0:T(2,128)(2,1)}, bf16[1,1,1536]{2,1,0:T(2,128)(2,1)S(1)}, u32[]{:S(2)}) copy-start(bf16[1,1,1536]{2,1,0:T(2,128)(2,1)S(1)} %collective-permute-done.13) | copy-start | bytes 9220
  63.6 5.8 %collective-permute-start.14 = (bf16[1,1,1536]{2,1,0:T(2,128)(2,1)S(1)}, bf16[1,1,1536]{2,1,0:T(2,128)(2,1)S(1)}, u32[]{:S(2)}, u32[]{:S(2)}) collective-permute-start(bf16[1,1,1536]{2,1,0:T(2,128)(2,1)S(1)} %collective-permute-done.13), channel_id=1, source_target_pairs={{0,2},{2,4},{4,6},{6,8},{8,10},{10,12},{12,14},{14,16},{16,18},{18... | collective-permute-start | bytes 9224 | tf_op jit(solution)/shard_map/ppermute | solution.py:76
  69.3 5.8 %collective-permute-start.15 = (bf16[1,1,1536]{2,1,0:T(2,128)(2,1)S(1)}, bf16[1,1,1536]{2,1,0:T(2,128)(2,1)S(1)}, u32[]{:S(2)}, u32[]{:S(2)}) collective-permute-start(bf16[1,1,1536]{2,1,0:T(2,128)(2,1)S(1)} %collective-permute-done.14), channel_id=1, source_target_pairs={{0,2},{2,4},{4,6},{6,8},{8,10},{10,12},{12,14},{14,16},{16,18},{18... | collective-permute-start | bytes 9224 | tf_op jit(solution)/shard_map/ppermute | solution.py:76
  69.4 23.3 %copy-start.17 = (bf16[1,1,1536]{2,1,0:T(2,128)(2,1)S(1)}, bf16[1,1,1536]{2,1,0:T(2,128)(2,1)}, u32[]{:S(2)}) copy-start(bf16[1,1,1536]{2,1,0:T(2,128)(2,1)} %copy-done.16) | copy-start | bytes 9220
  69.4 23.3 %copy-start.15 = (bf16[1,1,1536]{2,1,0:T(2,128)(2,1)S(1)}, bf16[1,1,1536]{2,1,0:T(2,128)(2,1)}, u32[]{:S(2)}) copy-start(bf16[1,1,1536]{2,1,0:T(2,128)(2,1)} %copy-done.14) | copy-start | bytes 9220
  69.4 23.3 %copy-start.13 = (bf16[1,1,1536]{2,1,0:T(2,128)(2,1)S(1)}, bf16[1,1,1536]{2,1,0:T(2,128)(2,1)}, u32[]{:S(2)}) copy-start(bf16[1,1,1536]{2,1,0:T(2,128)(2,1)} %copy-done.12) | copy-start | bytes 9220
  69.4 23.4 %copy-start.11 = (bf16[1,1,1536]{2,1,0:T(2,128)(2,1)S(1)}, bf16[1,1,1536]{2,1,0:T(2,128)(2,1)}, u32[]{:S(2)}) copy-start(bf16[1,1,1536]{2,1,0:T(2,128)(2,1)} %copy-done.10) | copy-start | bytes 9220
  69.4 23.4 %copy-start.9 = (bf16[1,1,1536]{2,1,0:T(2,128)(2,1)S(1)}, bf16[1,1,1536]{2,1,0:T(2,128)(2,1)}, u32[]{:S(2)}) copy-start(bf16[1,1,1536]{2,1,0:T(2,128)(2,1)} %copy-done.8) | copy-start | bytes 9220
  69.4 23.5 %copy-start.7 = (f32[1,1,1536]{2,1,0:T(1,128)S(1)}, f32[1,1,1536]{2,1,0:T(1,128)}, u32[]{:S(2)}) copy-start(f32[1,1,1536]{2,1,0:T(1,128)} %param.16) | copy-start | bytes 18436
  69.5 17.3 %copy-start.6 = (f32[3,17,16,128]{3,2,1,0:T(8,128)}, f32[3,17,16,128]{3,2,1,0:T(8,128)S(1)}, u32[]{:S(2)}) copy-start(f32[3,17,16,128]{3,2,1,0:T(8,128)S(1)} %get-tuple-element.38) | copy-start | bytes 1253380
  75.1 5.8 %collective-permute-start.16 = (bf16[1,1,1536]{2,1,0:T(2,128)(2,1)S(1)}, bf16[1,1,1536]{2,1,0:T(2,128)(2,1)S(1)}, u32[]{:S(2)}, u32[]{:S(2)}) collective-permute-start(bf16[1,1,1536]{2,1,0:T(2,128)(2,1)S(1)} %collective-permute-done.15), channel_id=1, source_target_pairs={{0,2},{2,4},{4,6},{6,8},{8,10},{10,12},{12,14},{14,16},{16,18},{18... | collective-permute-start | bytes 9224 | tf_op jit(solution)/shard_map/ppermute | solution.py:76
  75.9 5.0 %copy-start.4 = (f32[3,18,16,128]{3,2,1,0:T(8,128)}, f32[3,18,16,128]{3,2,1,0:T(8,128)S(1)}, u32[]{:S(2)}) copy-start(f32[3,18,16,128]{3,2,1,0:T(8,128)S(1)} %get-tuple-element.42) | copy-start | bytes 1327108
  80.9 5.9 %collective-permute-start.17 = (bf16[1,1,1536]{2,1,0:T(2,128)(2,1)S(1)}, bf16[1,1,1536]{2,1,0:T(2,128)(2,1)S(1)}, u32[]{:S(2)}, u32[]{:S(2)}) collective-permute-start(bf16[1,1,1536]{2,1,0:T(2,128)(2,1)S(1)} %collective-permute-done.16), channel_id=1, source_target_pairs={{0,2},{2,4},{4,6},{6,8},{8,10},{10,12},{12,14},{14,16},{16,18},{18... | collective-permute-start | bytes 9224 | tf_op jit(solution)/shard_map/ppermute | solution.py:76
  80.9 11.7 %copy-start.19 = (bf16[1,1,1536]{2,1,0:T(2,128)(2,1)S(1)}, bf16[1,1,1536]{2,1,0:T(2,128)(2,1)}, u32[]{:S(2)}) copy-start(bf16[1,1,1536]{2,1,0:T(2,128)(2,1)} %copy-done.18) | copy-start | bytes 9220
  80.9 33.3 %collective-permute-start.2 = (f32[3,18,1,128]{3,2,1,0:T(1,128)S(1)}, f32[3,18,1,128]{3,2,1,0:T(1,128)}, u32[]{:S(2)}, u32[]{:S(2)}) collective-permute-start(f32[3,18,1,128]{3,2,1,0:T(1,128)S(1)} %get-tuple-element.32), channel_id=1, source_target_pairs={{0,1},{2,3},{4,5},{6,7},{8,9},{10,11},{12,13},{14,15},{16,17},{18,... | collective-permute-start | bytes 82952 | tf_op jit(solution)/shard_map/ppermute | solution.py:14
  85.4 28.8 %collective-permute-start.3 = (f32[3,18,1,128]{3,2,1,0:T(1,128)S(1)}, f32[3,18,1,128]{3,2,1,0:T(1,128)}, u32[]{:S(2)}, u32[]{:S(2)}) collective-permute-start(f32[3,18,1,128]{3,2,1,0:T(1,128)S(1)} %get-tuple-element.33), channel_id=1, source_target_pairs={{1,0},{3,2},{5,4},{7,6},{9,8},{11,10},{13,12},{15,14},{17,16},{19,... | collective-permute-start | bytes 82952 | tf_op jit(solution)/shard_map/ppermute | solution.py:15
  86.7 5.8 %collective-permute-start.18 = (bf16[1,1,1536]{2,1,0:T(2,128)(2,1)S(1)}, bf16[1,1,1536]{2,1,0:T(2,128)(2,1)S(1)}, u32[]{:S(2)}, u32[]{:S(2)}) collective-permute-start(bf16[1,1,1536]{2,1,0:T(2,128)(2,1)S(1)} %collective-permute-done.17), channel_id=1, source_target_pairs={{0,2},{2,4},{4,6},{6,8},{8,10},{10,12},{12,14},{14,16},{16,18},{18... | collective-permute-start | bytes 9224 | tf_op jit(solution)/shard_map/ppermute | solution.py:76
  93.2 0.7 copy-start.21
  114.2 1.4 %copy-start.3 = (f32[3,3,16,16,128]{4,3,2,1,0:T(8,128)S(1)}, f32[3,3,16,16,128]{4,3,2,1,0:T(8,128)}, u32[]{:S(2)}) copy-start(f32[3,3,16,16,128]{4,3,2,1,0:T(8,128)} %param.14) | copy-start | bytes 3538948
  115.6 1.2 copy-start.5
